TPU v7x, 32 devices: a whole 2x2x4 slice. The times are simulated.
32 devices in a mesh: row: 8 (over z, y), col: 4 (over x, core).
Axes of the slice: x: 2, y: 2, z: 4, core: 2. Of those that a mesh axis runs over, the one named last changes fastest.
Arguments:
- three_centre: bfloat16 [192, 512, 512], P('row', 'col'), may hold values from -0.25 to 0.25
- tensor_pattern: int32 [192, 4, 4], P('row'), may hold values 0 or 1
- occ_density: bfloat16 [512, 512], P('row'), may hold values from -0.25 to 0.25
- virt_density: bfloat16 [512, 512], P('row'), may hold values from -0.25 to 0.25
- density_pattern: int32 [4, 4], replicated, may hold values 0 or 1
Outputs:
- response: float32 [192, 192], P('row')
All inputs are finite; a program needn't handle non-finite values. No bound on the sum of `tensor_pattern` on one device may be relied on, other than what follows from the above.
Results may differ from a plain program's by a relative error of at most 0.0041.
Values may be sent and summed in bfloat16 or wider, within the bound.
A program may use at most 64 MiB of HBM per device.

v0:
```python
import jax
import jax.numpy as jnp
from jax import lax
from jax.sharding import PartitionSpec as P

BS = 128


def expand_blocks(pattern, block_size, first, second):
    return jnp.repeat(jnp.repeat(pattern, block_size, first), block_size, second)


def per_device(three_centre, tensor_pattern, occ_density, virt_density, density_pattern):
    aux_count = three_centre.shape[0]
    local_rows = three_centre.shape[1]
    orbital_count = three_centre.shape[2]
    offset = lax.axis_index("col") * local_rows
    row_blocks = (offset + jnp.arange(local_rows, dtype=jnp.int32)) // BS
    pattern_rows = jnp.take(tensor_pattern, row_blocks, axis=1)
    tensor_mask = jnp.repeat(pattern_rows, BS, 2).astype(jnp.bfloat16)
    masked = three_centre * tensor_mask
    occupied_full, virtual_full = (
        lax.all_gather(occ_density, "row", axis=0, tiled=True),
        lax.all_gather(virt_density, "row", axis=0, tiled=True),
    )
    density_mask = expand_blocks(density_pattern, BS, 0, 1).astype(jnp.bfloat16)
    occupied = occupied_full * density_mask
    virtual = virtual_full * density_mask
    moved = jnp.dot(
        masked.reshape(aux_count * local_rows, orbital_count),
        virtual,
        preferred_element_type=jnp.float32,
    ).astype(jnp.bfloat16)
    moved = moved.reshape(aux_count, local_rows, orbital_count)
    moved_cols, regrouped = (
        lax.all_to_all(moved, "col", split_axis=2, concat_axis=1, tiled=True),
        lax.all_to_all(masked, "col", split_axis=2, concat_axis=1, tiled=True),
    )
    second = jnp.einsum(
        "lm,pms->pls", occupied, moved_cols, preferred_element_type=jnp.float32
    ).astype(jnp.bfloat16)
    grouped_left, grouped_right = (
        lax.all_to_all(second, "row", split_axis=1, concat_axis=0, tiled=True),
        lax.all_to_all(regrouped, "row", split_axis=1, concat_axis=0, tiled=True),
    )
    total_aux = grouped_left.shape[0]
    left_flat = grouped_left.reshape(total_aux, -1)
    right_flat = grouped_right.reshape(total_aux, -1)
    partial_chi = lax.dot_general(
        left_flat, right_flat, (((1,), (1,)), ((), ())), preferred_element_type=jnp.float32
    )
    row_summed = lax.psum_scatter(partial_chi, "row", scatter_dimension=0, tiled=True)
    return lax.psum(row_summed, "col")


def solution(mesh):
    in_specs = (P("row", "col", None), P("row", None, None), P("row", None), P("row", None), P())
    out_specs = P("row", None)
    return jax.shard_map(
        per_device, mesh=mesh, in_specs=in_specs, out_specs=out_specs, check_vma=False
    )
```

profile of v0, /device:TPU:0, one launch (start us, length us, event | category | flops | bytes accessed | tf_op | source)
XLA Modules:
  0.0 393.6 jit_solution(10314164889137517839)
XLA Ops:
  6.6 0.6 copy-done
  7.2 0.7 gather_fusion
  8.0 0.2 fusion.9
  8.2 1.5 copy.27
  9.7 5.4 %broadcast_in_dim.21 = bf16[24,128,4,128]{3,2,1,0:T(4,128)(2,1)} broadcast(bf16[24,128,4]{2,1,0:T(8,128)(2,1)S(1)} %copy.27), dimensions={0,1,2} | broadcast | bytes 3170304 | tf_op jit(solution)/shard_map/broadcast_in_dim | solution.py:20
  15.1 4.1 %convert_element_type.28 = bf16[24,128,512]{2,1,0:T(8,128)(2,1)S(1)} reshape(bf16[24,128,4,128]{3,2,1,0:T(4,128)(2,1)} %broadcast_in_dim.21) | data formatting | bytes 6291456 | tf_op jit(solution)/shard_map/convert_element_type | solution.py:20
  19.2 33.0 %all_gather.6 = bf16[512,512]{1,0:T(8,128)(2,1)S(1)} all-gather(bf16[64,512]{1,0:T(8,128)(2,1)S(1)} %copy-done.5), channel_id=1, replica_groups=mesh['row'=8,'col'=4] {'row'}, dimensions={0}, use_global_device_ids=true | all-gather | bytes 589824 | tf_op jit(solution)/shard_map/all_gather | solution.py:24
  52.2 3.0 mul.13
  55.2 0.6 broadcast_in_dim.23
  55.8 1.8 convolution_convert_fusion
  57.7 3.4 copy.28
  61.1 3.7 all-to-all-start
  64.8 4.8 %copy.33 = bf16[24,128,512]{1,0,2:T(8,128)(2,1)} copy(bf16[24,128,512]{2,1,0:T(8,128)(2,1)} %copy-done.2) | data formatting | bytes 6291456 | tf_op jit(solution)/shard_map/mul | solution.py:21
  69.6 32.0 %all-to-all-done = bf16[24,128,512]{1,0,2:T(8,128)(2,1)S(1)} async-done(((bf16[24,128,512]{1,0,2:T(8,128)(2,1)}), bf16[24,128,512]{1,0,2:T(8,128)(2,1)S(1)}, u32[]{:S(2)}, u32[]{:S(2)}) %all-to-all-start) | async-done | bytes 3145760 | tf_op jit(solution)/shard_map/all_to_all | solution.py:36
  101.7 1.7 copy-done.1
  103.3 3.7 all-to-all-start.2
  107.0 33.4 %all_gather.7 = bf16[512,512]{1,0:T(8,128)(2,1)} all-gather(bf16[64,512]{1,0:T(8,128)(2,1)S(1)} %copy-done.6), channel_id=1, replica_groups=mesh['row'=8,'col'=4] {'row'}, dimensions={0}, use_global_device_ids=true | all-gather | bytes 589824 | tf_op jit(solution)/shard_map/all_gather | solution.py:23
  140.5 6.0 %copy.61 = bf16[24,128,4,128]{1,2,3,0:T(4,128)(2,1)} copy(bf16[24,128,4,128]{1,0,3,2:T(8,128)(2,1)} %bitcast.49) | data formatting | bytes 6291456 | tf_op jit(solution)/shard_map/all_to_all | solution.py:36
  146.5 5.7 %all_to_all.51 = bf16[24,512,128]{1,2,0:T(8,128)(2,1)} reshape(bf16[24,4,128,128]{2,1,3,0:T(4,128)(2,1)} %bitcast.52) | data formatting | bytes 6291456 | tf_op jit(solution)/shard_map/all_to_all | solution.py:36
  152.2 5.7 %convert_bitcast_fusion = bf16[24,512,128]{1,2,0:T(8,128)(2,1)} fusion(bf16[24,512,128]{1,2,0:T(8,128)(2,1)} %all_to_all.51, bf16[512,512]{1,0:T(8,128)(2,1)} %all_gather.7, bf16[64,8,4,128]{3,2,1,0:T(4,128)(2,1)} %bitcast.58), kind=kOutput, calls=%fused_computation.8 | convolution fusion | flops 1612447744 | bytes 7340032 | tf_op jit(solution)/shard_map/lm,pms->pls/dot_general | solution.py:39
  157.9 4.8 %copy.30 = bf16[24,512,128]{2,0,1:T(8,128)(2,1)} copy(bf16[24,512,128]{1,2,0:T(8,128)(2,1)} %convert_bitcast_fusion) | data formatting | bytes 6291456 | tf_op jit(solution)/shard_map/convert_element_type | solution.py:41
  162.7 6.0 %all-to-all-start.1 = ((bf16[24,512,128]{2,0,1:T(8,128)(2,1)}), bf16[24,512,128]{2,0,1:T(8,128)(2,1)}, u32[]{:S(2)}, u32[]{:S(2)}) async-start(bf16[24,512,128]{2,0,1:T(8,128)(2,1)} %copy.30), calls=%async_computation.1 | async-start | bytes 6291456 | tf_op jit(solution)/shard_map/all_to_all | solution.py:43
  168.7 3.8 copy.40
  172.5 61.3 %all-to-all-done.1 = bf16[24,512,128]{2,0,1:T(8,128)(2,1)} async-done(((bf16[24,512,128]{2,0,1:T(8,128)(2,1)}), bf16[24,512,128]{2,0,1:T(8,128)(2,1)}, u32[]{:S(2)}, u32[]{:S(2)}) %all-to-all-start.1) | async-done | bytes 3145760 | tf_op jit(solution)/shard_map/all_to_all | solution.py:43
  233.8 3.6 all-to-all-start.3
  237.6 4.4 %copy.32 = bf16[8,24,64,128]{3,2,1,0:T(8,128)(2,1)} copy(bf16[8,24,64,128]{3,1,2,0:T(8,128)(2,1)} %bitcast.11) | data formatting | bytes 6291456 | tf_op jit(solution)/shard_map/all_to_all | solution.py:43
  242.0 66.2 %all-to-all-done.3 = bf16[24,512,128]{2,0,1:T(8,128)(2,1)S(1)} async-done(((bf16[24,512,128]{2,0,1:T(8,128)(2,1)}), bf16[24,512,128]{2,0,1:T(8,128)(2,1)S(1)}, u32[]{:S(2)}, u32[]{:S(2)}) %all-to-all-start.3) | async-done | bytes 3145760 | tf_op jit(solution)/shard_map/all_to_all | solution.py:44
  308.2 0.8 copy.37
  309.0 1.0 copy-done.3
  310.0 4.0 %fusion = f32[192,192]{1,0:T(8,128)} fusion(bf16[24,8,64,128]{3,2,1,0:T(8,128)(2,1)S(1)} %bitcast.55, bf16[24,8,64,128]{3,2,1,0:T(8,128)(2,1)S(1)} %bitcast.54), kind=kOutput, calls=%fused_computation.2 | convolution fusion | flops 603979776 | bytes 6438912 | tf_op jit(solution)/shard_map/dot_general | solution.py:49
  314.1 61.3 %reduce-scatter.2.cloned.1.call-done = f32[24,192]{1,0:T(8,128)} async-done(((f32[192,192]{1,0:T(8,128)}), f32[24,192]{1,0:T(8,128)}) %reduce-scatter.2.cloned.1.call-update) | async-done | bytes 18448 | tf_op jit(solution)/shard_map/reduce_scatter | solution.py:52
  375.4 11.4 %psum.7 = f32[24,192]{1,0:T(8,128)} all-reduce(f32[24,192]{1,0:T(8,128)} %reduce-scatter.2.cloned.1.call-done), channel_id=1, replica_groups=mesh['row'=8,'col'=4] {'col'}, use_global_device_ids=true, to_apply=%region_1.2 | all-reduce | flops 4608 | bytes 36864 | tf_op jit(solution)/shard_map/psum | solution.py:53
  (21 shorter events, 0.1 us)
Async XLA Ops:
  6.5 0.7 copy-start
  15.1 4.1 %copy-start.7 = (s32[4,4]{1,0:T(4,128)S(1)}, s32[4,4]{1,0:T(4,128)}, u32[]{:S(2)}) copy-start(s32[4,4]{1,0:T(4,128)} %param.9) | copy-start | bytes 196
  15.1 4.1 %copy-start.5 = (bf16[64,512]{1,0:T(8,128)(2,1)S(1)}, bf16[64,512]{1,0:T(8,128)(2,1)}, u32[]{:S(2)}) copy-start(bf16[64,512]{1,0:T(8,128)(2,1)} %param.8) | copy-start | bytes 196612
  55.2 2.5 copy-start.2
  55.8 1.8 copy-start.4
  61.1 40.6 %all-to-all-start = ((bf16[24,128,512]{1,0,2:T(8,128)(2,1)}), bf16[24,128,512]{1,0,2:T(8,128)(2,1)S(1)}, u32[]{:S(2)}, u32[]{:S(2)}) async-start(bf16[24,128,512]{1,0,2:T(8,128)(2,1)} %copy.28), calls=%async_computation | async-start | bytes 6291456 | tf_op jit(solution)/shard_map/all_to_all | solution.py:36
  69.6 37.4 %copy-start.6 = (bf16[64,512]{1,0:T(8,128)(2,1)S(1)}, bf16[64,512]{1,0:T(8,128)(2,1)}, u32[]{:S(2)}) copy-start(bf16[64,512]{1,0:T(8,128)(2,1)} %param.7) | copy-start | bytes 196612
  101.7 1.7 copy-start.1
  103.3 59.4 %all-to-all-start.2 = ((bf16[24,128,512]{1,0,2:T(8,128)(2,1)}), bf16[24,128,512]{1,0,2:T(8,128)(2,1)S(1)}, u32[]{:S(2)}, u32[]{:S(2)}) async-start(bf16[24,128,512]{1,0,2:T(8,128)(2,1)} %copy.33), calls=%async_computation.2 | async-start | bytes 6291456 | tf_op jit(solution)/shard_map/all_to_all | solution.py:37
  162.7 71.1 %all-to-all-start.1 = ((bf16[24,512,128]{2,0,1:T(8,128)(2,1)}), bf16[24,512,128]{2,0,1:T(8,128)(2,1)}, u32[]{:S(2)}, u32[]{:S(2)}) async-start(bf16[24,512,128]{2,0,1:T(8,128)(2,1)} %copy.30), calls=%async_computation.1 | async-start | bytes 6291456 | tf_op jit(solution)/shard_map/all_to_all | solution.py:43
  233.8 74.3 %all-to-all-start.3 = ((bf16[24,512,128]{2,0,1:T(8,128)(2,1)}), bf16[24,512,128]{2,0,1:T(8,128)(2,1)S(1)}, u32[]{:S(2)}, u32[]{:S(2)}) async-start(bf16[24,512,128]{2,0,1:T(8,128)(2,1)} %bitcast.50), calls=%async_computation.3 | async-start | bytes 6291456 | tf_op jit(solution)/shard_map/all_to_all | solution.py:44
  237.5 137.9 %reduce-scatter.2.cloned.1.call-start = ((), (), s32[]{:S(2)}) async-start(), calls=%async_computation.5 | async-start | bytes 221184 | tf_op jit(solution)/shard_map/reduce_scatter | solution.py:52
  308.2 1.9 copy-start.3
Sparse Core Ops, SparseCore 0:
  314.2 61.0 reduce-scatter.1
where the time goes:
time: 395 us; the launch traced here: 394 us
  waiting for transfers between devices  221 us (56%)
  blocking collectives  77.8 us (20%)
  local copies, waits for them, and re-layouts  49.5 us (13%)
  starting transfers between devices  17.1 us (4%)
  between operations  13.6 us (3%)
  matrix products  11.6 us (3%)
    all_to_all x1, waiting for transfers between devices, per_device(): lax.all_to_all(regrouped, 'row', split_axis=1, concat_axis=0, tiled=True)  66.2 us
    all_to_all x1, waiting for transfers between devices, per_device(): lax.all_to_all(second, 'row', split_axis=1, concat_axis=0, tiled=True)  61.3 us
    reduce_scatter x1, waiting for transfers between devices, per_device(): lax.psum_scatter(partial_chi, 'row', scatter_dimension=0, tiled=True)  61.3 us
    all_gather x1, blocking collectives, per_device(): lax.all_gather(occ_density, 'row', axis=0, tiled=True)  33.4 us
    all_gather x1, blocking collectives, per_device(): lax.all_gather(virt_density, 'row', axis=0, tiled=True)  33 us
    all_to_all x1, waiting for transfers between devices, per_device(): lax.all_to_all(moved, 'col', split_axis=2, concat_axis=1, tiled=True)  32 us
    all_to_all x2, local copies, waits for them, and re-layouts, per_device(): lax.all_to_all(moved, 'col', split_axis=2, concat_axis=1, tiled=True)  11.7 us
    psum x1, blocking collectives, per_device(): return lax.psum(row_summed, 'col')  11.4 us
  transfers between devices with their start and end apart: 5, of which 4 were waited for; matrix products, arithmetic and copies ran while one was open for 8% of the time, Pallas kernels for 0%

commit v1 on v0

--- a/solution.py
+++ b/solution.py
@@ -1,16 +1,274 @@
+import functools
+
 import jax
 import jax.numpy as jnp
 from jax import lax
+from jax.experimental import pallas as pl
+from jax.experimental.pallas import tpu as pltpu
 from jax.sharding import PartitionSpec as P
 
 BS = 128
+MESH = pl.DeviceIdType.MESH
 
 
 def expand_blocks(pattern, block_size, first, second):
     return jnp.repeat(jnp.repeat(pattern, block_size, first), block_size, second)
 
 
-def per_device(three_centre, tensor_pattern, occ_density, virt_density, density_pattern):
+def far_first(count):
+    return sorted(range(1, count), key=lambda k: (abs(k - count / 2), k))
+
+
+def greet(me_row, me_col, rows, cols):
+    barrier = pltpu.get_barrier_semaphore()
+    for i in range(rows):
+        for j in range(cols):
+            if i or j:
+                pl.semaphore_signal(
+                    barrier,
+                    inc=1,
+                    device_id=(lax.rem(me_row + i, rows), lax.rem(me_col + j, cols)),
+                    device_id_type=MESH,
+                )
+    pl.semaphore_wait(barrier, rows * cols - 1)
+
+
+def exchange_kernel(
+    rows, cols,
+    tensor_ref, pattern_ref, occ_ref, virt_ref, density_ref,
+    b_out, s_out,
+    masked, virt_all, occ_all, moved, moved_cols, second,
+    gather_send, gather_recv, spread_send, spread_recv,
+    b_send, b_recv, m_send, m_recv, s_send, s_recv, own_sem,
+):
+    me_row, me_col = lax.axis_index("row"), lax.axis_index("col")
+    aux, local, orb = tensor_ref.shape
+    strip = local // rows
+    wide = orb // cols
+    blocks = orb // BS
+    quarter = virt_ref.shape[0] // cols
+    row_steps = far_first(rows)
+
+    def remote(src, dst, send, recv, to_row, to_col):
+        copy = pltpu.make_async_remote_copy(
+            src_ref=src, dst_ref=dst, send_sem=send, recv_sem=recv,
+            device_id=(to_row, to_col), device_id_type=MESH,
+        )
+        copy.start()
+        return copy
+
+    greet(me_row, me_col, rows, cols)
+
+    share = pl.ds(pl.multiple_of(me_col * quarter, quarter), quarter)
+    gathers = []
+    owns = []
+    for d, (src, dst) in enumerate(((virt_ref, virt_all), (occ_ref, occ_all))):
+        own = pltpu.make_async_copy(src.at[share], dst.at[me_row, me_col], own_sem.at[d])
+        own.start()
+        owns.append(own)
+        gathers.append([
+            remote(src.at[share], dst.at[me_row, me_col],
+                   gather_send.at[d, k], gather_recv.at[d, k],
+                   lax.rem(me_row + k, rows), me_col)
+            for k in row_steps
+        ])
+
+    block_row = (me_col * local) // BS
+
+    def mask_one(p, carry):
+        for j in range(blocks):
+            keep = pattern_ref[(p * blocks + block_row) * blocks + j].astype(jnp.float32)
+            piece = tensor_ref[p, :, j * BS:(j + 1) * BS].astype(jnp.float32)
+            masked[p, :, j * BS:(j + 1) * BS] = (piece * keep).astype(jnp.bfloat16)
+        return carry
+
+    lax.fori_loop(0, aux, mask_one, 0)
+
+    b_copies = []
+    for k in row_steps:
+        to_row = lax.rem(me_row + k, rows)
+        part = pl.ds(pl.multiple_of(to_row * strip, strip), strip)
+        b_copies.append(remote(masked.at[:, part, :], b_out.at[me_row],
+                               b_send.at[k], b_recv.at[k], to_row, me_col))
+    own_part = pl.ds(pl.multiple_of(me_row * strip, strip), strip)
+    own_b = pltpu.make_async_copy(masked.at[:, own_part, :], b_out.at[me_row], own_sem.at[2])
+    own_b.start()
+
+    spreads = []
+    for d, full in enumerate((virt_all, occ_all)):
+        owns[d].wait()
+        for copy in gathers[d]:
+            copy.wait_recv()
+        spreads.append([
+            remote(full.at[:, me_col], full.at[:, me_col],
+                   spread_send.at[d, k], spread_recv.at[d, k],
+                   me_row, lax.rem(me_col + k, cols))
+            for k in range(1, cols)
+        ])
+
+    def take_density(full, d):
+        for copy in spreads[d]:
+            copy.wait()
+        for copy in gathers[d]:
+            copy.wait_send()
+        values = full[...].reshape(orb, orb)
+        lines = []
+        for i in range(blocks):
+            line = []
+            for j in range(blocks):
+                keep = density_ref[i * blocks + j].astype(jnp.float32)
+                piece = values[i * BS:(i + 1) * BS, j * BS:(j + 1) * BS].astype(jnp.float32)
+                line.append((piece * keep).astype(jnp.bfloat16))
+            lines.append(jnp.concatenate(line, axis=1))
+        full[...] = jnp.concatenate(lines, axis=0).reshape(full.shape)
+
+    take_density(virt_all, 0)
+
+    def move_one(p, carry):
+        product = jnp.dot(masked[p], virt_all[...].reshape(orb, orb),
+                          preferred_element_type=jnp.float32).astype(jnp.bfloat16)
+        for j in range(cols):
+            moved[j, p] = product[:, j * wide:(j + 1) * wide]
+        return carry
+
+    lax.fori_loop(0, aux, move_one, 0)
+
+    m_copies = []
+    for k in range(1, cols):
+        to_col = lax.rem(me_col + k, cols)
+        m_copies.append(remote(moved.at[to_col], moved_cols.at[me_col],
+                               m_send.at[k], m_recv.at[k], me_row, to_col))
+    own_m = pltpu.make_async_copy(moved.at[me_col], moved_cols.at[me_col], own_sem.at[3])
+    own_m.start()
+
+    take_density(occ_all, 1)
+    own_m.wait()
+    for copy in m_copies:
+        copy.wait()
+
+    def second_two(p, carry):
+        rhs = jnp.concatenate(
+            [moved_cols[:, 2 * p + h].reshape(orb, wide) for h in range(2)], axis=1)
+        product = jnp.dot(occ_all[...].reshape(orb, orb), rhs,
+                          preferred_element_type=jnp.float32).astype(jnp.bfloat16)
+        for h in range(2):
+            second[2 * p + h] = product[:, h * wide:(h + 1) * wide]
+        return carry
+
+    lax.fori_loop(0, aux // 2, second_two, 0)
+
+    lanes = pl.ds(pl.multiple_of(me_col * wide, wide), wide)
+
+    def strip_of(to_row, to_col):
+        return pl.ds(pl.multiple_of(to_col * local + to_row * strip, strip), strip)
+
+    s_copies = []
+    for k in row_steps + [0]:
+        for q in range(cols):
+            if k or q:
+                to_row, to_col = lax.rem(me_row + k, rows), lax.rem(me_col + q, cols)
+                s_copies.append(remote(
+                    second.at[:, strip_of(to_row, to_col), :],
+                    s_out.at[me_row, :, :, lanes],
+                    s_send.at[k, q], s_recv.at[k, q], to_row, to_col))
+    own_s = pltpu.make_async_copy(second.at[:, strip_of(me_row, me_col), :],
+                                  s_out.at[me_row, :, :, lanes], own_sem.at[4])
+    own_s.start()
+
+    own_b.wait()
+    for copy in b_copies:
+        copy.wait()
+    own_s.wait()
+    for copy in s_copies:
+        copy.wait()
+
+
+def sum_kernel(rows, cols, part_ref, out_ref, landed, total, others,
+               row_send, row_recv, col_send, col_recv):
+    me_row, me_col = lax.axis_index("row"), lax.axis_index("col")
+    greet(me_row, me_col, rows, cols)
+    copies = []
+    for k in far_first(rows):
+        to_row = lax.rem(me_row + k, rows)
+        copy = pltpu.make_async_remote_copy(
+            src_ref=part_ref.at[to_row], dst_ref=landed.at[k],
+            send_sem=row_send.at[k], recv_sem=row_recv.at[k],
+            device_id=(to_row, me_col), device_id_type=MESH)
+        copy.start()
+        copies.append(copy)
+    for copy in copies:
+        copy.wait()
+    value = part_ref[me_row]
+    for k in range(1, rows):
+        value = value + landed[k]
+    total[...] = value
+    copies = []
+    for k in range(1, cols):
+        to_col = lax.rem(me_col + k, cols)
+        copy = pltpu.make_async_remote_copy(
+            src_ref=total, dst_ref=others.at[me_col],
+            send_sem=col_send.at[k], recv_sem=col_recv.at[k],
+            device_id=(me_row, to_col), device_id_type=MESH)
+        copy.start()
+        copies.append(copy)
+    others[me_col] = total[...]
+    for copy in copies:
+        copy.wait()
+    value = others[0]
+    for k in range(1, cols):
+        value = value + others[k]
+    out_ref[...] = value
+
+
+def direct(rows, cols, three_centre, tensor_pattern, occ_density, virt_density, density_pattern):
+    aux, local, orb = three_centre.shape
+    strip, wide = local // rows, orb // cols
+    quarter = occ_density.shape[0] // cols
+    bf16 = jnp.bfloat16
+    dma = pltpu.SemaphoreType.DMA
+    vmem = pl.BlockSpec(memory_space=pltpu.VMEM)
+    smem = pl.BlockSpec(memory_space=pltpu.SMEM)
+    landed = jax.ShapeDtypeStruct((rows, aux, strip, orb), bf16)
+    b_all, s_all = pl.pallas_call(
+        functools.partial(exchange_kernel, rows, cols),
+        out_shape=(landed, landed),
+        in_specs=[vmem, smem, vmem, vmem, smem],
+        out_specs=(pl.BlockSpec(memory_space=pl.ANY),) * 2,
+        scratch_shapes=[
+            pltpu.VMEM((aux, local, orb), bf16),
+            pltpu.VMEM((rows, cols, quarter, orb), bf16),
+            pltpu.VMEM((rows, cols, quarter, orb), bf16),
+            pltpu.VMEM((cols, aux, local, wide), bf16),
+            pltpu.VMEM((cols, aux, local, wide), bf16),
+            pltpu.VMEM((aux, orb, wide), bf16),
+            dma((2, rows)), dma((2, rows)), dma((2, cols)), dma((2, cols)),
+            dma((rows,)), dma((rows,)), dma((cols,)), dma((cols,)),
+            dma((rows, cols)), dma((rows, cols)), dma((5,)),
+        ],
+        compiler_params=pltpu.CompilerParams(
+            collective_id=0, has_side_effects=True, vmem_limit_bytes=40 * 2**20),
+    )(three_centre, tensor_pattern.reshape(-1), occ_density, virt_density,
+      density_pattern.reshape(-1))
+    total = rows * aux
+    partial_chi = lax.dot_general(
+        s_all.reshape(total, strip, orb), b_all.reshape(total, strip, orb),
+        (((1, 2), (1, 2)), ((), ())), preferred_element_type=jnp.float32)
+    return pl.pallas_call(
+        functools.partial(sum_kernel, rows, cols),
+        out_shape=jax.ShapeDtypeStruct((aux, total), jnp.float32),
+        in_specs=[vmem],
+        out_specs=vmem,
+        scratch_shapes=[
+            pltpu.VMEM((rows, aux, total), jnp.float32),
+            pltpu.VMEM((aux, total), jnp.float32),
+            pltpu.VMEM((cols, aux, total), jnp.float32),
+            dma((rows,)), dma((rows,)), dma((cols,)), dma((cols,)),
+        ],
+        compiler_params=pltpu.CompilerParams(collective_id=1, has_side_effects=True),
+    )(partial_chi.reshape(rows, aux, total))
+
+
+def staged(three_centre, tensor_pattern, occ_density, virt_density, density_pattern):
     aux_count = three_centre.shape[0]
     local_rows = three_centre.shape[1]
     orbital_count = three_centre.shape[2]
@@ -54,6 +312,17 @@
 
 
 def solution(mesh):
+    rows, cols = mesh.shape["row"], mesh.shape["col"]
+
+    def per_device(three_centre, tensor_pattern, occ_density, virt_density, density_pattern):
+        aux, local, orb = three_centre.shape
+        aligned = (
+            local % (16 * rows) == 0 and occ_density.shape[0] % (16 * cols) == 0
+            and orb % (128 * cols) == 0 and BS % local == 0 and aux % 8 == 0
+        )
+        args = (three_centre, tensor_pattern, occ_density, virt_density, density_pattern)
+        return direct(rows, cols, *args) if aligned else staged(*args)
+
     in_specs = (P("row", "col", None), P("row", None, None), P("row", None), P("row", None), P())
     out_specs = P("row", None)
     return jax.shard_map(

time: 395 us -> 200 us (0.51)
  waiting for transfers between devices: 221 us -> 0 us
  Pallas kernels: 0 us -> 185 us
  blocking collectives: 77.8 us -> 0 us
  local copies, waits for them, and re-layouts: 49.5 us -> 6.59 us
  starting transfers between devices: 17.1 us -> 0 us
  between operations: 13.6 us -> 0.03 us
    pallas_call x0 -> x2, Pallas kernels: none -> 185 us  [the longest x1 155 us: direct(): pl.pallas_call(functools.partial(exchange_kernel, rows, cols), out_shape=...]
    all_to_all x4 -> x0, waiting for transfers between devices: 160 us -> none  [the longest x1 66.2 us: per_device(): lax.all_to_all(regrouped, 'row', split_axis=1, concat_axis=0, tiled=True)]
    all_gather x2 -> x0, blocking collectives: 66.5 us -> none  [the longest x1 33.4 us: per_device(): lax.all_gather(occ_density, 'row', axis=0, tiled=True)]
    reduce_scatter x1 -> x0, waiting for transfers between devices: 61.3 us -> none  [per_device(): lax.psum_scatter(partial_chi, 'row', scatter_dimension=0, tiled=True)]
    all_to_all x5 -> x0, local copies, waits for them, and re-layouts: 20.8 us -> none  [the longest x2 11.7 us: per_device(): lax.all_to_all(moved, 'col', split_axis=2, concat_axis=1, tiled=True)]
    all_to_all x4 -> x0, starting transfers between devices: 17 us -> none  [the longest x1 5.97 us: per_device(): lax.all_to_all(second, 'row', split_axis=1, concat_axis=0, tiled=True)]
    psum x1 -> x0, blocking collectives: 11.4 us -> none  [per_device(): return lax.psum(row_summed, 'col')]
    convert_element_type x3 -> x0, local copies, waits for them, and re-layouts: 10.4 us -> none  [the longest x2 5.54 us: per_device(): tensor_mask = jnp.repeat(pattern_rows, BS, 2).astype(jnp.bfloat16)]
  transfers between devices with their start and end apart: 5 -> 0, of which waited for: 4 -> 0; matrix products, arithmetic and copies ran while one was open for 8% -> 0% of each run, Pallas kernels for 0% -> 0%
where the time goes in v1:
time: 200 us
  Pallas kernels  185 us (92%)
  matrix products  7.99 us (4%)
  local copies, waits for them, and re-layouts  6.59 us (3%)
    pallas_call x1, Pallas kernels, direct(): pl.pallas_call(functools.partial(exchange_kernel, rows, cols), out_shape=...  155 us
    pallas_call x1, Pallas kernels, direct(): pl.pallas_call(functools.partial(sum_kernel, rows, cols), out_shape=jax.S...  29.7 us
    dot_general x1, matrix products, direct(): lax.dot_general(s_all.reshape(total, strip, orb), b_all.reshape(total, st...  7.99 us
    unnamed x8, local copies, waits for them, and re-layouts  5.71 us

profile of v1, /device:TPU:0, one launch (start us, length us, event | category | flops | bytes accessed | tf_op | source)
XLA Modules:
  0.0 199.7 jit_solution(2041512372363047258)
XLA Ops:
  0.0 0.8 reshape.14.density_ref
  0.8 0.8 copy.8
  1.6 0.1 reshape.13.pattern_ref
  1.7 0.0 copy-start
  1.7 1.9 copy-done
  3.6 0.0 copy-start.1
  3.6 0.8 copy-done.1
  4.4 0.0 copy-start.2
  4.4 0.8 copy-done.2
  5.3 155.4 %shard_map.55 = (bf16[8,24,16,512]{3,2,1,0:T(8,128)(2,1)S(1)}, bf16[8,24,16,512]{3,2,1,0:T(8,128)(2,1)S(1)}) custom-call(bf16[24,128,512]{2,1,0:T(8,128)(2,1)S(1)} %copy-done, s32[384]{0:T(512)S(1)} %reshape.13.pattern_ref, bf16[64,512]{1,0:T(8,128)(2,1)S(1)} %copy-done.1, bf16[64,512]{1,0:T(8,128)(2,1)S(1)} %copy-done.2, s32[16]{0:T(128)S(1)} %reshape.14.density_ref), custom_call_target="tpu_custom_call" | custom-call | tf_op jit(solution)/shard_map/pallas_call | solution.py:232
  160.7 8.0 %fusion.4.part_ref = f32[8,24,192]{2,1,0:T(8,128)} fusion(bf16[192,16,512]{2,1,0:T(8,128)(2,1)S(1)} %bitcast.9, bf16[8,24,16,512]{3,2,1,0:T(8,128)(2,1)S(1)} %get-tuple-element.7), kind=kOutput, calls=%fused_computation.4 | convolution fusion | flops 603979776 | bytes 6438912 | tf_op jit(solution)/shard_map/dot_general | solution.py:253
  168.7 29.7 %shard_map.56 = f32[24,192]{1,0:T(8,128)} custom-call(f32[8,24,192]{2,1,0:T(8,128)} %fusion.4.part_ref), custom_call_target="tpu_custom_call" | custom-call | tf_op jit(solution)/shard_map/pallas_call | solution.py:256
  198.4 1.3 copy.23
Async XLA Ops:
  1.7 1.9 copy-start
  3.6 0.8 copy-start.1
  4.4 0.8 copy-start.2

commit v2 on v1

--- a/solution.py
+++ b/solution.py
@@ -15,8 +15,20 @@
     return jnp.repeat(jnp.repeat(pattern, block_size, first), block_size, second)
 
 
-def far_first(count):
-    return sorted(range(1, count), key=lambda k: (abs(k - count / 2), k))
+def partner(me, k, count):
+    if count & (count - 1):
+        return lax.rem(me + k, count), lax.rem(me + count - k, count)
+    bit, other = 1, me
+    while bit < count:
+        if k & bit:
+            other = other + bit - 2 * bit * ((me // bit) % 2)
+        bit *= 2
+    return other, other
+
+
+def near_first(count):
+    half = [k for k in range(2, count // 2)]
+    return half + [1] * (count > 1) + [k for k in range(max(2, count // 2), count)]
 
 
 def greet(me_row, me_col, rows, cols):
@@ -34,12 +46,12 @@
 
 
 def exchange_kernel(
-    rows, cols,
+    rows, cols, chunks,
     tensor_ref, pattern_ref, occ_ref, virt_ref, density_ref,
     b_out, s_out,
     masked, virt_all, occ_all, moved, moved_cols, second,
     gather_send, gather_recv, spread_send, spread_recv,
-    b_send, b_recv, m_send, m_recv, s_send, s_recv, own_sem,
+    b_send, b_recv, m_send, m_recv, s_send, s_recv, own_sem, load_sem,
 ):
     me_row, me_col = lax.axis_index("row"), lax.axis_index("col")
     aux, local, orb = tensor_ref.shape
@@ -47,7 +59,7 @@
     wide = orb // cols
     blocks = orb // BS
     quarter = virt_ref.shape[0] // cols
-    row_steps = far_first(rows)
+    row_steps = near_first(rows)
 
     def remote(src, dst, send, recv, to_row, to_col):
         copy = pltpu.make_async_remote_copy(
@@ -57,6 +69,8 @@
         copy.start()
         return copy
 
+    load = pltpu.make_async_copy(tensor_ref, masked, load_sem)
+    load.start()
     greet(me_row, me_col, rows, cols)
 
     share = pl.ds(pl.multiple_of(me_col * quarter, quarter), quarter)
@@ -69,7 +83,7 @@
         gathers.append([
             remote(src.at[share], dst.at[me_row, me_col],
                    gather_send.at[d, k], gather_recv.at[d, k],
-                   lax.rem(me_row + k, rows), me_col)
+                   partner(me_row, k, rows)[0], me_col)
             for k in row_steps
         ])
 
@@ -77,16 +91,17 @@
 
     def mask_one(p, carry):
         for j in range(blocks):
-            keep = pattern_ref[(p * blocks + block_row) * blocks + j].astype(jnp.float32)
-            piece = tensor_ref[p, :, j * BS:(j + 1) * BS].astype(jnp.float32)
+            keep = pattern_ref[block_row, j, p].astype(jnp.float32)
+            piece = masked[p, :, j * BS:(j + 1) * BS].astype(jnp.float32)
             masked[p, :, j * BS:(j + 1) * BS] = (piece * keep).astype(jnp.bfloat16)
         return carry
 
+    load.wait()
     lax.fori_loop(0, aux, mask_one, 0)
 
     b_copies = []
     for k in row_steps:
-        to_row = lax.rem(me_row + k, rows)
+        to_row = partner(me_row, k, rows)[0]
         part = pl.ds(pl.multiple_of(to_row * strip, strip), strip)
         b_copies.append(remote(masked.at[:, part, :], b_out.at[me_row],
                                b_send.at[k], b_recv.at[k], to_row, me_col))
@@ -102,7 +117,7 @@
         spreads.append([
             remote(full.at[:, me_col], full.at[:, me_col],
                    spread_send.at[d, k], spread_recv.at[d, k],
-                   me_row, lax.rem(me_col + k, cols))
+                   me_row, partner(me_col, k, cols)[0])
             for k in range(1, cols)
         ])
 
@@ -116,7 +131,7 @@
         for i in range(blocks):
             line = []
             for j in range(blocks):
-                keep = density_ref[i * blocks + j].astype(jnp.float32)
+                keep = density_ref[i, j].astype(jnp.float32)
                 piece = values[i * BS:(i + 1) * BS, j * BS:(j + 1) * BS].astype(jnp.float32)
                 line.append((piece * keep).astype(jnp.bfloat16))
             lines.append(jnp.concatenate(line, axis=1))
@@ -131,20 +146,22 @@
             moved[j, p] = product[:, j * wide:(j + 1) * wide]
         return carry
 
-    lax.fori_loop(0, aux, move_one, 0)
-
+    span = aux // chunks
     m_copies = []
-    for k in range(1, cols):
-        to_col = lax.rem(me_col + k, cols)
-        m_copies.append(remote(moved.at[to_col], moved_cols.at[me_col],
-                               m_send.at[k], m_recv.at[k], me_row, to_col))
-    own_m = pltpu.make_async_copy(moved.at[me_col], moved_cols.at[me_col], own_sem.at[3])
-    own_m.start()
+    for h in range(chunks):
+        lax.fori_loop(h * span, (h + 1) * span, move_one, 0)
+        piece = pl.ds(h * span, span)
+        copies = []
+        for k in range(1, cols):
+            to_col = partner(me_col, k, cols)[0]
+            copies.append(remote(moved.at[to_col, piece], moved_cols.at[me_col, piece],
+                                 m_send.at[h, k], m_recv.at[h, k], me_row, to_col))
+        own = pltpu.make_async_copy(moved.at[me_col, piece], moved_cols.at[me_col, piece],
+                                    own_sem.at[5 + h])
+        own.start()
+        m_copies.append(copies + [own])
 
     take_density(occ_all, 1)
-    own_m.wait()
-    for copy in m_copies:
-        copy.wait()
 
     def second_two(p, carry):
         rhs = jnp.concatenate(
@@ -155,22 +172,25 @@
             second[2 * p + h] = product[:, h * wide:(h + 1) * wide]
         return carry
 
-    lax.fori_loop(0, aux // 2, second_two, 0)
-
     lanes = pl.ds(pl.multiple_of(me_col * wide, wide), wide)
 
     def strip_of(to_row, to_col):
         return pl.ds(pl.multiple_of(to_col * local + to_row * strip, strip), strip)
 
     s_copies = []
-    for k in row_steps + [0]:
-        for q in range(cols):
-            if k or q:
-                to_row, to_col = lax.rem(me_row + k, rows), lax.rem(me_col + q, cols)
-                s_copies.append(remote(
-                    second.at[:, strip_of(to_row, to_col), :],
-                    s_out.at[me_row, :, :, lanes],
-                    s_send.at[k, q], s_recv.at[k, q], to_row, to_col))
+    for h in range(chunks):
+        piece = pl.ds(h * span, span)
+        for copy in m_copies[h]:
+            copy.wait()
+        lax.fori_loop(h * span // 2, (h + 1) * span // 2, second_two, 0)
+        for k in row_steps + [0]:
+            for q in range(cols):
+                if k or q:
+                    to_row, to_col = partner(me_row, k, rows)[0], partner(me_col, q, cols)[0]
+                    s_copies.append(remote(
+                        second.at[piece, strip_of(to_row, to_col), :],
+                        s_out.at[me_row, piece, :, lanes],
+                        s_send.at[h, k, q], s_recv.at[h, k, q], to_row, to_col))
     own_s = pltpu.make_async_copy(second.at[:, strip_of(me_row, me_col), :],
                                   s_out.at[me_row, :, :, lanes], own_sem.at[4])
     own_s.start()
@@ -188,8 +208,8 @@
     me_row, me_col = lax.axis_index("row"), lax.axis_index("col")
     greet(me_row, me_col, rows, cols)
     copies = []
-    for k in far_first(rows):
-        to_row = lax.rem(me_row + k, rows)
+    for k in near_first(rows):
+        to_row = partner(me_row, k, rows)[0]
         copy = pltpu.make_async_remote_copy(
             src_ref=part_ref.at[to_row], dst_ref=landed.at[k],
             send_sem=row_send.at[k], recv_sem=row_recv.at[k],
@@ -204,7 +224,7 @@
     total[...] = value
     copies = []
     for k in range(1, cols):
-        to_col = lax.rem(me_col + k, cols)
+        to_col = partner(me_col, k, cols)[0]
         copy = pltpu.make_async_remote_copy(
             src_ref=total, dst_ref=others.at[me_col],
             send_sem=col_send.at[k], recv_sem=col_recv.at[k],
@@ -225,14 +245,16 @@
     strip, wide = local // rows, orb // cols
     quarter = occ_density.shape[0] // cols
     bf16 = jnp.bfloat16
+    chunks = max(n for n in (1, 2, 3, 4) if aux % (2 * n) == 0)
     dma = pltpu.SemaphoreType.DMA
     vmem = pl.BlockSpec(memory_space=pltpu.VMEM)
     smem = pl.BlockSpec(memory_space=pltpu.SMEM)
+    hbm = pl.BlockSpec(memory_space=pltpu.MemorySpace.HBM)
     landed = jax.ShapeDtypeStruct((rows, aux, strip, orb), bf16)
     b_all, s_all = pl.pallas_call(
-        functools.partial(exchange_kernel, rows, cols),
+        functools.partial(exchange_kernel, rows, cols, chunks),
         out_shape=(landed, landed),
-        in_specs=[vmem, smem, vmem, vmem, smem],
+        in_specs=[hbm, smem, hbm, hbm, smem],
         out_specs=(pl.BlockSpec(memory_space=pl.ANY),) * 2,
         scratch_shapes=[
             pltpu.VMEM((aux, local, orb), bf16),
@@ -242,13 +264,13 @@
             pltpu.VMEM((cols, aux, local, wide), bf16),
             pltpu.VMEM((aux, orb, wide), bf16),
             dma((2, rows)), dma((2, rows)), dma((2, cols)), dma((2, cols)),
-            dma((rows,)), dma((rows,)), dma((cols,)), dma((cols,)),
-            dma((rows, cols)), dma((rows, cols)), dma((5,)),
+            dma((rows,)), dma((rows,)), dma((chunks, cols)), dma((chunks, cols)),
+            dma((chunks, rows, cols)), dma((chunks, rows, cols)), dma((5 + chunks,)), dma(()),
         ],
         compiler_params=pltpu.CompilerParams(
-            collective_id=0, has_side_effects=True, vmem_limit_bytes=40 * 2**20),
-    )(three_centre, tensor_pattern.reshape(-1), occ_density, virt_density,
-      density_pattern.reshape(-1))
+            collective_id=0, has_side_effects=True, vmem_limit_bytes=67_000_000),
+    )(three_centre, tensor_pattern.transpose(1, 2, 0), occ_density, virt_density,
+      density_pattern)
     total = rows * aux
     partial_chi = lax.dot_general(
         s_all.reshape(total, strip, orb), b_all.reshape(total, strip, orb),

time: 200 us -> 184 us (0.920)
  Pallas kernels: 185 us -> 171 us
  local copies, waits for them, and re-layouts: 6.59 us -> 1.35 us
  matrix products: 7.99 us -> 10.8 us
    pallas_call x1, Pallas kernels: 29.7 us -> 18.4 us  [direct(): pl.pallas_call(functools.partial(sum_kernel, rows, cols), out_shape=jax.S...]
    unnamed x8 -> x1, local copies, waits for them, and re-layouts: 5.71 us -> 1.35 us
    dot_general x1, matrix products: 7.99 us -> 10.8 us  [direct(): lax.dot_general(s_all.reshape(total, strip, orb), b_all.reshape(total, st...]
    pallas_call x1, Pallas kernels: 155 us -> 153 us  [direct(): pl.pallas_call(functools.partial(exchange_kernel, rows, cols, chunks), ou...]
where the time goes in v2:
time: 184 us; the launch traced here: 183 us
  Pallas kernels  171 us (93%)
  matrix products  10.8 us (6%)
    pallas_call x1, Pallas kernels, direct(): pl.pallas_call(functools.partial(exchange_kernel, rows, cols, chunks), ou...  153 us
    pallas_call x1, Pallas kernels, direct(): pl.pallas_call(functools.partial(sum_kernel, rows, cols), out_shape=jax.S...  18.4 us
    dot_general x1, matrix products, direct(): lax.dot_general(s_all.reshape(total, strip, orb), b_all.reshape(total, st...  10.8 us

profile of v2, /device:TPU:0, one launch (start us, length us, event | category | flops | bytes accessed | tf_op | source)
XLA Modules:
  0.0 183.4 jit_solution(18052698333846346921)
XLA Ops:
  0.0 152.7 %shard_map.55 = (bf16[8,24,16,512]{3,2,1,0:T(8,128)(2,1)}, bf16[8,24,16,512]{3,2,1,0:T(8,128)(2,1)}) custom-call(bf16[24,128,512]{2,1,0:T(8,128)(2,1)} %tensor_ref.1, s32[4,4,24]{2,1,0:T(4,128)} %bitcast.10, bf16[64,512]{1,0:T(8,128)(2,1)} %occ_ref.1, bf16[64,512]{1,0:T(8,128)(2,1)} %virt_ref.1, s32[4,4]{1,0:T(4,128)} %density_ref.1), custom_call_target="tpu_custom_call" | custom-call | tf_op jit(solution)/shard_map/pallas_call | solution.py:254
  152.7 10.8 %fusion.4.part_ref = f32[8,24,192]{2,1,0:T(8,128)} fusion(bf16[192,16,512]{2,1,0:T(8,128)(2,1)} %bitcast.11, bf16[8,24,16,512]{3,2,1,0:T(8,128)(2,1)} %get-tuple-element.7), kind=kOutput, calls=%fused_computation.4 | convolution fusion | flops 603979776 | bytes 6438912 | tf_op jit(solution)/shard_map/dot_general | solution.py:275
  163.6 18.4 %shard_map.56 = f32[24,192]{1,0:T(8,128)} custom-call(f32[8,24,192]{2,1,0:T(8,128)} %fusion.4.part_ref), custom_call_target="tpu_custom_call" | custom-call | tf_op jit(solution)/shard_map/pallas_call | solution.py:278
  182.0 1.3 copy.20

commit v3 on v2

--- a/solution.py
+++ b/solution.py
@@ -48,10 +48,11 @@
 def exchange_kernel(
     rows, cols, chunks,
     tensor_ref, pattern_ref, occ_ref, virt_ref, density_ref,
-    b_out, s_out,
+    out_ref,
+    b_in, s_in, b_lines, wide_rows, part, landed, total, others,
     masked, virt_all, occ_all, moved, moved_cols, second,
     gather_send, gather_recv, spread_send, spread_recv,
-    b_send, b_recv, m_send, m_recv, s_send, s_recv, own_sem, load_sem,
+    b_send, b_recv, m_send, m_recv, s_send, s_recv, own_sem, load_sem, row_send, row_recv, col_send, col_recv,
 ):
     me_row, me_col = lax.axis_index("row"), lax.axis_index("col")
     aux, local, orb = tensor_ref.shape
@@ -102,11 +103,11 @@
     b_copies = []
     for k in row_steps:
         to_row = partner(me_row, k, rows)[0]
-        part = pl.ds(pl.multiple_of(to_row * strip, strip), strip)
-        b_copies.append(remote(masked.at[:, part, :], b_out.at[me_row],
+        theirs = pl.ds(pl.multiple_of(to_row * strip, strip), strip)
+        b_copies.append(remote(masked.at[:, theirs, :], b_in.at[me_row],
                                b_send.at[k], b_recv.at[k], to_row, me_col))
     own_part = pl.ds(pl.multiple_of(me_row * strip, strip), strip)
-    own_b = pltpu.make_async_copy(masked.at[:, own_part, :], b_out.at[me_row], own_sem.at[2])
+    own_b = pltpu.make_async_copy(masked.at[:, own_part, :], b_in.at[me_row], own_sem.at[2])
     own_b.start()
 
     spreads = []
@@ -177,7 +178,7 @@
     def strip_of(to_row, to_col):
         return pl.ds(pl.multiple_of(to_col * local + to_row * strip, strip), strip)
 
-    s_copies = []
+    s_copies = [[] for _ in range(chunks)]
     for h in range(chunks):
         piece = pl.ds(h * span, span)
         for copy in m_copies[h]:
@@ -187,51 +188,65 @@
             for q in range(cols):
                 if k or q:
                     to_row, to_col = partner(me_row, k, rows)[0], partner(me_col, q, cols)[0]
-                    s_copies.append(remote(
+                    s_copies[h].append(remote(
                         second.at[piece, strip_of(to_row, to_col), :],
-                        s_out.at[me_row, piece, :, lanes],
+                        s_in.at[me_row, piece, :, lanes],
                         s_send.at[h, k, q], s_recv.at[h, k, q], to_row, to_col))
     own_s = pltpu.make_async_copy(second.at[:, strip_of(me_row, me_col), :],
-                                  s_out.at[me_row, :, :, lanes], own_sem.at[4])
+                                  s_in.at[me_row, :, :, lanes], own_sem.at[4])
     own_s.start()
+
+    def widen(p, carry):
+        rows_at = pl.ds(pl.multiple_of(p * aux * strip, aux * strip), aux * strip)
+        for j in range(orb // BS):
+            wide_rows[j, rows_at, :] = b_in[p, :, :, j * BS:(j + 1) * BS].reshape(
+                aux * strip, BS).astype(jnp.float32)
+        return carry
+
+    def every(line, count):
+        return jnp.concatenate(
+            [wide_rows[j, pl.ds(line, count, stride=strip), :] for j in range(orb // BS)],
+            axis=1).astype(jnp.bfloat16)
 
     own_b.wait()
     for copy in b_copies:
         copy.wait()
+    lax.fori_loop(0, rows, widen, 0)
+    for line in range(strip):
+        b_lines[line] = every(line, rows * aux)
+
     own_s.wait()
-    for copy in s_copies:
-        copy.wait()
-
-
-def sum_kernel(rows, cols, part_ref, out_ref, landed, total, others,
-               row_send, row_recv, col_send, col_recv):
-    me_row, me_col = lax.axis_index("row"), lax.axis_index("col")
-    greet(me_row, me_col, rows, cols)
+    for h in range(chunks):
+        for copy in s_copies[h]:
+            copy.wait()
+        count = rows * span
+        for j in range(orb // BS):
+            wide_rows[j, 0:count * strip, :] = s_in[
+                :, h * span:(h + 1) * span, :, j * BS:(j + 1) * BS].reshape(
+                count * strip, BS).astype(jnp.float32)
+        chi = jnp.zeros((count, rows * aux), jnp.float32)
+        for line in range(strip):
+            chi = chi + lax.dot_general(every(line, count), b_lines[line], (((1,), (1,)), ((), ())),
+                                        preferred_element_type=jnp.float32)
+        part[:, h * span:(h + 1) * span, :] = chi.reshape(rows, span, rows * aux)
+
     copies = []
-    for k in near_first(rows):
+    for k in row_steps:
         to_row = partner(me_row, k, rows)[0]
-        copy = pltpu.make_async_remote_copy(
-            src_ref=part_ref.at[to_row], dst_ref=landed.at[k],
-            send_sem=row_send.at[k], recv_sem=row_recv.at[k],
-            device_id=(to_row, me_col), device_id_type=MESH)
-        copy.start()
-        copies.append(copy)
+        copies.append(remote(part.at[to_row], landed.at[k],
+                             row_send.at[k], row_recv.at[k], to_row, me_col))
+    value = part[me_row]
     for copy in copies:
         copy.wait()
-    value = part_ref[me_row]
     for k in range(1, rows):
         value = value + landed[k]
     total[...] = value
     copies = []
     for k in range(1, cols):
         to_col = partner(me_col, k, cols)[0]
-        copy = pltpu.make_async_remote_copy(
-            src_ref=total, dst_ref=others.at[me_col],
-            send_sem=col_send.at[k], recv_sem=col_recv.at[k],
-            device_id=(me_row, to_col), device_id_type=MESH)
-        copy.start()
-        copies.append(copy)
-    others[me_col] = total[...]
+        copies.append(remote(total, others.at[me_col],
+                             col_send.at[k], col_recv.at[k], me_row, to_col))
+    others[me_col] = value
     for copy in copies:
         copy.wait()
     value = others[0]
@@ -245,18 +260,27 @@
     strip, wide = local // rows, orb // cols
     quarter = occ_density.shape[0] // cols
     bf16 = jnp.bfloat16
-    chunks = max(n for n in (1, 2, 3, 4) if aux % (2 * n) == 0)
+    chunks = aux // 8
+    total = rows * aux
+    f32 = jnp.float32
     dma = pltpu.SemaphoreType.DMA
     vmem = pl.BlockSpec(memory_space=pltpu.VMEM)
     smem = pl.BlockSpec(memory_space=pltpu.SMEM)
     hbm = pl.BlockSpec(memory_space=pltpu.MemorySpace.HBM)
-    landed = jax.ShapeDtypeStruct((rows, aux, strip, orb), bf16)
-    b_all, s_all = pl.pallas_call(
+    return pl.pallas_call(
         functools.partial(exchange_kernel, rows, cols, chunks),
-        out_shape=(landed, landed),
+        out_shape=jax.ShapeDtypeStruct((aux, total), f32),
         in_specs=[hbm, smem, hbm, hbm, smem],
-        out_specs=(pl.BlockSpec(memory_space=pl.ANY),) * 2,
+        out_specs=vmem,
         scratch_shapes=[
+            pltpu.VMEM((rows, aux, strip, orb), bf16),
+            pltpu.VMEM((rows, aux, strip, orb), bf16),
+            pltpu.VMEM((strip, total, orb), bf16),
+            pltpu.VMEM((orb // BS, total * strip, BS), f32),
+            pltpu.VMEM((rows, aux, total), f32),
+            pltpu.VMEM((rows, aux, total), f32),
+            pltpu.VMEM((aux, total), f32),
+            pltpu.VMEM((cols, aux, total), f32),
             pltpu.VMEM((aux, local, orb), bf16),
             pltpu.VMEM((rows, cols, quarter, orb), bf16),
             pltpu.VMEM((rows, cols, quarter, orb), bf16),
@@ -266,28 +290,12 @@
             dma((2, rows)), dma((2, rows)), dma((2, cols)), dma((2, cols)),
             dma((rows,)), dma((rows,)), dma((chunks, cols)), dma((chunks, cols)),
             dma((chunks, rows, cols)), dma((chunks, rows, cols)), dma((5 + chunks,)), dma(()),
+            dma((rows,)), dma((rows,)), dma((cols,)), dma((cols,)),
         ],
         compiler_params=pltpu.CompilerParams(
             collective_id=0, has_side_effects=True, vmem_limit_bytes=67_000_000),
     )(three_centre, tensor_pattern.transpose(1, 2, 0), occ_density, virt_density,
       density_pattern)
-    total = rows * aux
-    partial_chi = lax.dot_general(
-        s_all.reshape(total, strip, orb), b_all.reshape(total, strip, orb),
-        (((1, 2), (1, 2)), ((), ())), preferred_element_type=jnp.float32)
-    return pl.pallas_call(
-        functools.partial(sum_kernel, rows, cols),
-        out_shape=jax.ShapeDtypeStruct((aux, total), jnp.float32),
-        in_specs=[vmem],
-        out_specs=vmem,
-        scratch_shapes=[
-            pltpu.VMEM((rows, aux, total), jnp.float32),
-            pltpu.VMEM((aux, total), jnp.float32),
-            pltpu.VMEM((cols, aux, total), jnp.float32),
-            dma((rows,)), dma((rows,)), dma((cols,)), dma((cols,)),
-        ],
-        compiler_params=pltpu.CompilerParams(collective_id=1, has_side_effects=True),
-    )(partial_chi.reshape(rows, aux, total))
 
 
 def staged(three_centre, tensor_pattern, occ_density, virt_density, density_pattern):

time: 184 us -> 172 us (0.935)
  matrix products: 10.8 us -> 0 us
    pallas_call x1 -> x0, Pallas kernels: 18.4 us -> none  [direct(): pl.pallas_call(functools.partial(sum_kernel, rows, cols), out_shape=jax.S...]
    pallas_call x1, Pallas kernels: 153 us -> 171 us  [direct(): pl.pallas_call(functools.partial(exchange_kernel, rows, cols, chunks), ou...]
    dot_general x1 -> x0, matrix products: 10.8 us -> none  [direct(): lax.dot_general(s_all.reshape(total, strip, orb), b_all.reshape(total, st...]
where the time goes in v3:
time: 172 us
  Pallas kernels  171 us (99%)
    pallas_call x1, Pallas kernels, direct(): pl.pallas_call(functools.partial(exchange_kernel, rows, cols, chunks), ou...  171 us

profile of v3, /device:TPU:0, one launch (start us, length us, event | category | flops | bytes accessed | tf_op | source)
XLA Modules:
  0.0 172.1 jit_solution(11172961386272846131)
XLA Ops:
  0.0 170.7 %shard_map.55 = f32[24,192]{1,0:T(8,128)} custom-call(bf16[24,128,512]{2,1,0:T(8,128)(2,1)} %tensor_ref.1, s32[4,4,24]{2,1,0:T(4,128)} %bitcast.1, bf16[64,512]{1,0:T(8,128)(2,1)} %occ_ref.1, bf16[64,512]{1,0:T(8,128)(2,1)} %virt_ref.1, s32[4,4]{1,0:T(4,128)} %density_ref.1), custom_call_target="tpu_custom_call" | custom-call | tf_op jit(solution)/shard_map/pallas_call | solution.py:270
  170.7 1.3 copy.7

commit v4 on v3

--- a/solution.py
+++ b/solution.py
@@ -184,7 +184,7 @@
         for copy in m_copies[h]:
             copy.wait()
         lax.fori_loop(h * span // 2, (h + 1) * span // 2, second_two, 0)
-        for k in row_steps + [0]:
+        for k in [0] + row_steps:
             for q in range(cols):
                 if k or q:
                     to_row, to_col = partner(me_row, k, rows)[0], partner(me_col, q, cols)[0]

time: 172 us -> 171 us (level)
  Pallas kernels: 171 us -> 169 us
where the time goes in v4:
time: 171 us
  Pallas kernels  169 us (99%)
    pallas_call x1, Pallas kernels, direct(): pl.pallas_call(functools.partial(exchange_kernel, rows, cols, chunks), ou...  169 us

profile of v4, /device:TPU:0, one launch (start us, length us, event | category | flops | bytes accessed | tf_op | source)
XLA Modules:
  0.0 170.8 jit_solution(7975253339654034421)
XLA Ops:
  0.0 169.4 %shard_map.55 = f32[24,192]{1,0:T(8,128)} custom-call(bf16[24,128,512]{2,1,0:T(8,128)(2,1)} %tensor_ref.1, s32[4,4,24]{2,1,0:T(4,128)} %bitcast.1, bf16[64,512]{1,0:T(8,128)(2,1)} %occ_ref.1, bf16[64,512]{1,0:T(8,128)(2,1)} %virt_ref.1, s32[4,4]{1,0:T(4,128)} %density_ref.1), custom_call_target="tpu_custom_call" | custom-call | tf_op jit(solution)/shard_map/pallas_call | solution.py:270
  169.4 1.3 copy.7
